TPU v7x, 32 devices: a whole 2x2x4 slice. The times are simulated.
32 devices in a mesh: seq: 16 (over z, y, x), head: 2 (over core).
Axes of the slice: x: 2, y: 2, z: 4, core: 2. Of those that a mesh axis runs over, the one named last changes fastest.
Arguments:
- query_raw: bfloat16 [2048, 2048], P('seq', 'head'), may hold values from -6 to 6
- key_raw: bfloat16 [2048, 2048], P('seq', 'head'), may hold values from -6 to 6
- value_raw: bfloat16 [2048, 2048], P('seq', 'head'), may hold values from -6 to 6
- gate_raw: float32 [2048, 2048], P('seq', 'head')
- beta_raw: float32 [2048, 16], P('seq', 'head'), may hold values from -8.5 to 3.5
- conv_weight: float32 [3, 4, 2048], P(None, None, 'head'), may hold values from -3 to 3
- decay_log: float32 [2048], P('head')
- grad_out: bfloat16 [2048, 2048], P('seq', 'head'), may hold values from -6 to 6
Outputs:
- query_grad: bfloat16 [2048, 2048], P('seq', 'head')
- key_grad: bfloat16 [2048, 2048], P('seq', 'head')
- value_grad: bfloat16 [2048, 2048], P('seq', 'head')
- gate_grad: float32 [2048, 2048], P('seq', 'head')
- beta_grad: float32 [2048, 16], P('seq', 'head')
- conv_grad: float32 [3, 4, 2048], P(None, None, 'head')
- decay_grad: float32 [2048], P('head')
All inputs are finite; a program needn't handle non-finite values.
Results may differ from a plain program's by a relative error of at most 0.0018.
Values may be sent and summed in bfloat16 or wider, within the bound.
A program may use at most 128 MiB of HBM per device.

v0:
```python
import functools

import jax
import jax.numpy as jnp
from jax import lax
from jax.experimental import pallas as pl
from jax.experimental.pallas import tpu as pltpu
from jax.sharding import PartitionSpec as P

F32 = jnp.float32
BF16 = jnp.bfloat16
EPS = 1e-06
PAD = 8
RED = 16
GROUP = 2
VMEM_LIMIT = 60 * 1024 * 1024


def split(x):
    hi = x.astype(BF16)
    return hi, (x - hi.astype(F32)).astype(BF16)


def mm(a, b, ta=False, tb=False):
    ah, al = split(a)
    bh, bl = split(b)
    lhs = jnp.concatenate([ah, al], 0 if ta else 1)
    if tb:
        rhs = jnp.concatenate(
            [jnp.concatenate([bh, bh], 1), jnp.concatenate([bl, bl], 1)], 0
        )
    else:
        row = jnp.concatenate([bh, bl], 1)
        rhs = jnp.concatenate([row, row], 0)
    out = lax.dot_general(
        lhs,
        rhs,
        (((0 if ta else 1,), (1 if tb else 0,)), ((), ())),
        preferred_element_type=F32,
    )
    n = out.shape[1] // 2
    return out[:, :n] + out[:, n:]


def ones_mm(ones, x):
    hi, mid = split(x)
    low = (x - hi.astype(F32) - mid.astype(F32)).astype(BF16)
    n = x.shape[1]
    out = jnp.dot(
        ones.astype(BF16), jnp.concatenate([hi, mid, low], 1), preferred_element_type=F32
    )
    return out[:, :n] + out[:, n : 2 * n] + out[:, 2 * n :]


def sigmoid(x):
    return 1.0 / (1.0 + jnp.exp(-x))


def softplus(x):
    return jnp.maximum(x, 0.0) + jnp.log1p(jnp.exp(-jnp.abs(x)))


def iotas(size):
    r = lax.broadcasted_iota(jnp.int32, (size, size), 0)
    c = lax.broadcasted_iota(jnp.int32, (size, size), 1)
    return r, c


def conv_pre(ext, x_ref, halo_ref, w_ref, j, cols):
    size = x_ref.shape[0]
    ext[0:PAD, :] = halo_ref[j, :, cols].astype(F32)
    ext[PAD : PAD + size, :] = x_ref[:, cols].astype(F32)
    taps = w_ref.shape[1]
    rows = [ext[PAD - taps + 1 + i : PAD - taps + 1 + i + size, :] for i in range(taps)]
    pre = w_ref[j, 0:1, cols] * rows[0]
    for i in range(1, taps):
        pre = pre + w_ref[j, i : i + 1, cols] * rows[i]
    return pre, rows


def pick_column(ref, index):
    block = ref[...]
    lane = lax.broadcasted_iota(jnp.int32, block.shape, 1)
    return jnp.sum(jnp.where(lane == index, block, 0.0), axis=1, keepdims=True)


def unit(x):
    r = lax.rsqrt(jnp.sum(x * x, axis=1, keepdims=True) + EPS)
    return x * r, r


def decays(gate, dlog):
    size = gate.shape[0]
    half = size // 2
    r, c = iotas(size)
    speed = -jnp.exp(dlog)
    ld = speed * softplus(gate)
    cum = ones_mm(jnp.where(r >= c, 1.0, 0.0), ld)
    row = lax.broadcasted_iota(jnp.int32, gate.shape, 0)
    first = row < half
    mid = jnp.where(
        first, cum[half // 2 : half // 2 + 1, :], cum[half + half // 2 : half + half // 2 + 1, :]
    )
    edge = cum[half - 1 : half, :]
    last = cum[size - 1 : size, :]
    up = jnp.exp(cum - mid)
    down = jnp.exp(mid - cum)
    cross = jnp.exp(jnp.where(first, edge - cum, cum - edge))
    full = jnp.exp(cum)
    end = jnp.exp(last - cum)
    return ld, speed, up, down, cross, full, end, jnp.exp(last), first


def pair_scores(qk_up, k_down, qk_cross, k_cross):
    size = k_down.shape[0]
    half = size // 2
    same = mm(qk_up, k_down, tb=True)
    other = mm(qk_cross, k_cross, tb=True)
    r, c = iotas(size)
    same_half = (r < half) == (c < half)
    return (
        jnp.where(same_half, same[:size], other[:size]),
        jnp.where(same_half, same[size:], other[size:]),
    )


def unit_inverse(a):
    size = a.shape[0]
    r, c = iotas(size)
    ident = jnp.where(r == c, 1.0, 0.0)
    shift = 3
    small = jnp.where((r >> shift) == (c >> shift), a, 0.0)
    p2 = mm(small, small)
    base = ident - small
    base = base + mm(base, p2)
    p4 = mm(p2, p2)
    d = base + mm(base, p4)
    while (1 << shift) < size:
        joined = ((r >> (shift + 1)) == (c >> (shift + 1))) & ((r >> shift) != (c >> shift))
        d = d - mm(d, mm(jnp.where(joined, a, 0.0), d))
        shift += 1
    return d


def maps_kernel(
    group,
    q_ref, k_ref, v_ref, halo_ref, gate_ref, beta_ref, w_ref, dlog_ref, grad_ref,
    trans_ref, offset_ref, adjoint_ref, inv_ref, raw_ref, att_ref, reach_ref,
    ext,
):
    size = q_ref.shape[0]
    width = trans_ref.shape[1]
    r, c = iotas(size)
    for g in range(group):
        cols = slice(g * width, (g + 1) * width)
        head = pl.program_id(0) * group + g
        pre_q, _ = conv_pre(ext.at[3 * g], q_ref, halo_ref, w_ref, 0, cols)
        pre_k, _ = conv_pre(ext.at[3 * g + 1], k_ref, halo_ref, w_ref, 1, cols)
        pre_v, _ = conv_pre(ext.at[3 * g + 2], v_ref, halo_ref, w_ref, 2, cols)
        q, _ = unit(pre_q * sigmoid(pre_q))
        k, _ = unit(pre_k * sigmoid(pre_k))
        v = pre_v * sigmoid(pre_v)
        beta = sigmoid(pick_column(beta_ref, head))
        ld, speed, up, down, cross, full, end, dend, first = decays(
            gate_ref[:, cols], dlog_ref[:, cols]
        )
        kc = k * cross
        qk_up = jnp.concatenate([q * up, k * up], 0)
        qk_cross = jnp.concatenate([q * cross, kc], 0)
        att, raw = pair_scores(qk_up, k * down, qk_cross, kc)
        att = jnp.where(r >= c, att, 0.0)
        raw = jnp.where(r > c, raw, 0.0)
        inv = unit_inverse(raw * beta)
        by = mm(inv, jnp.concatenate([beta * k * full, beta * v], 1))
        by_k = by[:, :width]
        ends = mm(k * end, by, ta=True)
        rr, cc = iotas(width)
        trans_ref[g] = jnp.where(rr == cc, dend, 0.0) - ends[:, :width]
        offset_ref[g] = ends[:, width:]
        grad = grad_ref[:, cols].astype(F32)
        reach = mm(att, grad, ta=True)
        adjoint_ref[g] = mm(
            jnp.concatenate([q * full, -by_k], 0), jnp.concatenate([grad, reach], 0), ta=True
        )
        inv_ref[g] = inv
        raw_ref[g] = raw
        att_ref[g] = att
        reach_ref[g] = reach


def chain_kernel(
    trans_ref, offset_ref, adjoint_ref, state_ref, cotan_ref,
    send_s, recv_s, send_g, recv_g, ss, rs, sg, rg,
):
    n = lax.axis_size("seq")
    me = lax.axis_index("seq")
    right = lax.rem(me + 1, n)
    left = lax.rem(me + n - 1, n)
    heads = trans_ref.shape[0]
    barrier = pltpu.get_barrier_semaphore()
    for peer in (left, right):
        pl.semaphore_signal(
            barrier, inc=1, device_id={"seq": peer}, device_id_type=pl.DeviceIdType.MESH
        )
    pl.semaphore_wait(barrier, 2)

    def state_copy(h):
        return pltpu.make_async_remote_copy(
            src_ref=send_s.at[h], dst_ref=recv_s.at[h], send_sem=ss.at[h], recv_sem=rs.at[h],
            device_id={"seq": right}, device_id_type=pl.DeviceIdType.MESH,
        )

    def cotan_copy(h):
        return pltpu.make_async_remote_copy(
            src_ref=send_g.at[h], dst_ref=recv_g.at[h], send_sem=sg.at[h], recv_sem=rg.at[h],
            device_id={"seq": left}, device_id_type=pl.DeviceIdType.MESH,
        )

    def forward():
        @pl.loop(0, heads)
        def _(h):
            @pl.when(me == 0)
            def _():
                state_ref[h] = jnp.zeros_like(state_ref[h])
                send_s[h] = offset_ref[h]

            @pl.when(me > 0)
            def _():
                state_copy(h).wait_recv()
                state = recv_s[h]
                state_ref[h] = state
                send_s[h] = mm(trans_ref[h], state) + offset_ref[h]

            @pl.when(me < n - 1)
            def _():
                state_copy(h).start()

    def backward():
        @pl.loop(0, heads)
        def _(h):
            @pl.when(me == n - 1)
            def _():
                cotan_ref[h] = jnp.zeros_like(cotan_ref[h])
                send_g[h] = adjoint_ref[h]

            @pl.when(me < n - 1)
            def _():
                cotan_copy(h).wait_recv()
                cotan = recv_g[h]
                cotan_ref[h] = cotan
                send_g[h] = mm(trans_ref[h], cotan, ta=True) + adjoint_ref[h]

            @pl.when(me > 0)
            def _():
                cotan_copy(h).start()

    @pl.when(me < n // 2)
    def _():
        forward()
        backward()

    @pl.when(me >= n // 2)
    def _():
        backward()
        forward()

    @pl.loop(0, heads)
    def _(h):
        @pl.when(me < n - 1)
        def _():
            state_copy(h).wait_send()

        @pl.when(me > 0)
        def _():
            cotan_copy(h).wait_send()


def grads_kernel(
    group,
    q_ref, k_ref, v_ref, halo_ref, gate_ref, beta_ref, w_ref, dlog_ref, grad_ref,
    inv_ref, raw_ref, att_ref, reach_ref, state_ref, cotan_ref,
    dq_ref, dk_ref, dv_ref, dgate_ref, dbeta_ref, red_ref, tail_ref, last_ref,
    ext, dext,
):
    size = q_ref.shape[0]
    half = size // 2
    width = state_ref.shape[1]
    taps = w_ref.shape[1]
    r, c = iotas(size)
    same_half = (r < half) == (c < half)
    for g in range(group):
        cols = slice(g * width, (g + 1) * width)
        head = pl.program_id(0) * group + g
        pres, rows = [], []
        for j, ref in enumerate((q_ref, k_ref, v_ref)):
            pre, row = conv_pre(ext.at[3 * g + j], ref, halo_ref, w_ref, j, cols)
            pres.append(pre)
            rows.append(row)
        sig = [sigmoid(pre) for pre in pres]
        q, q_r = unit(pres[0] * sig[0])
        k, k_r = unit(pres[1] * sig[1])
        v = pres[2] * sig[2]
        beta = sigmoid(pick_column(beta_ref, head))
        gate = gate_ref[:, cols]
        ld, speed, up, down, cross, full, end, dend, first = decays(gate, dlog_ref[:, cols])
        inv, raw, att, reach = inv_ref[g], raw_ref[g], att_ref[g], reach_ref[g]
        state, cotan = state_ref[g], cotan_ref[g]
        grad = grad_ref[:, cols].astype(F32)

        resid = v - mm(k * full, state)
        deltas = mm(inv, beta * resid)
        d_deltas = reach + mm(k * end, cotan)
        d_err = mm(inv, d_deltas, ta=True)
        d_v = beta * d_err
        stacked = jnp.concatenate([grad, -d_v], 0)
        to_full = mm(stacked, state, tb=True)
        d_qf, d_kf = to_full[:size], to_full[size:]
        scores = mm(jnp.concatenate([grad, -d_err], 0), deltas, tb=True)
        d_att = jnp.where(r >= c, scores[:size], 0.0)
        d_coup = jnp.where(r > c, scores[size:], 0.0)
        d_ke = mm(deltas, cotan, tb=True)
        d_beta = jnp.sum(d_err * resid, axis=1, keepdims=True) + jnp.sum(
            d_coup * raw, axis=1, keepdims=True
        )
        d_raw = d_coup * beta
        kc = k * cross
        both = jnp.concatenate([d_att, d_raw], 0)
        same2 = jnp.concatenate([same_half, same_half], 0)
        d_same = jnp.where(same2, both, 0.0)
        d_other = jnp.where(same2, 0.0, both)
        from_same = mm(d_same, k * down)
        from_other = mm(d_other, kc)
        to_down = mm(d_same, jnp.concatenate([q * up, k * up], 0), ta=True)
        to_cross = mm(d_other, jnp.concatenate([q * cross, kc], 0), ta=True)
        d_q = from_same[:size] * up + from_other[:size] * cross + d_qf * full
        d_k_up = from_same[size:] * up + from_other[size:] * cross + d_kf * full
        k_end_part = d_ke * end
        d_k_down = to_down * down + to_cross * cross + k_end_part
        d_k = d_k_up + d_k_down
        d_cum = q * d_q + k * (d_k_up - d_k_down)
        ones_row = jnp.ones((8, width), F32)
        end_state = mm(ones_row, state * cotan, tb=True)[0:1, :]
        d_last = jnp.sum(k * k_end_part, axis=0, keepdims=True) + dend * end_state
        d_ld = ones_mm(jnp.where(c >= r, 1.0, 0.0), d_cum) + d_last
        dgate_ref[:, cols] = speed * sigmoid(gate) * d_ld
        d_dlog = jnp.sum(ld * d_ld, axis=0, keepdims=True)
        d_braw = d_beta * beta * (1.0 - beta)
        lane = lax.broadcasted_iota(jnp.int32, dbeta_ref.shape, 1)
        dbeta_ref[...] = jnp.where(lane == head, d_braw, dbeta_ref[...])

        d_q = q_r * (d_q - q * jnp.sum(q * d_q, axis=1, keepdims=True))
        d_k = k_r * (d_k - k * jnp.sum(k * d_k, axis=1, keepdims=True))
        red = []
        for j, (d_act, out_ref) in enumerate(((d_q, dq_ref), (d_k, dk_ref), (d_v, dv_ref))):
            s = sig[j]
            d_pre = d_act * (s * (1.0 + pres[j] * (1.0 - s)))
            spot = dext.at[3 * g + j]
            spot[0:PAD, :] = jnp.zeros((PAD, width), F32)
            spot[PAD : PAD + size, :] = d_pre
            spot[PAD + size :, :] = jnp.zeros((PAD, width), F32)
            whole = None
            tail = None
            for i in range(taps):
                w = w_ref[j, i : i + 1, cols]
                start = PAD + taps - 1 - i
                term = w * spot[start : start + size, :]
                edge = w * spot[taps - 1 - i : taps - 1 - i + PAD, :]
                whole = term if whole is None else whole + term
                tail = edge if tail is None else tail + edge
                red.append(jnp.sum(d_pre * rows[j][i], axis=0, keepdims=True))
            out_ref[:, cols] = whole.astype(BF16)
            tail_ref[j, :, cols] = tail
            last_ref[j, :, cols] = whole[size - PAD :, :]
        red.append(d_dlog)
        red.append(jnp.zeros((RED - len(red), width), F32))
        red_ref[g * RED : (g + 1) * RED, :] = jnp.concatenate(red, 0)


def finish_kernel(
    red_ref, tail_ref, total_ref, after_ref,
    parts, mine, result, tail_in, s1, r1, s2, r2, st, rt,
):
    n = lax.axis_size("seq")
    me = lax.axis_index("seq")
    owners = min(n, red_ref.shape[0] // 8)
    piece = red_ref.shape[0] // owners
    right = lax.rem(me + 1, n)
    left = lax.rem(me + n - 1, n)
    mesh_id = pl.DeviceIdType.MESH
    barrier = pltpu.get_barrier_semaphore()

    @pl.loop(1, n)
    def _(step):
        pl.semaphore_signal(
            barrier, inc=1, device_id={"seq": lax.rem(me + step, n)}, device_id_type=mesh_id
        )

    pl.semaphore_wait(barrier, n - 1)

    def rows(owner):
        return pl.ds(pl.multiple_of(owner * piece, 8), piece)

    tail_copy = pltpu.make_async_remote_copy(
        src_ref=tail_ref, dst_ref=tail_in, send_sem=st, recv_sem=rt,
        device_id={"seq": left}, device_id_type=mesh_id,
    )

    def scatter(owner, source):
        return pltpu.make_async_remote_copy(
            src_ref=red_ref.at[rows(owner)], dst_ref=parts.at[source],
            send_sem=s1.at[owner], recv_sem=r1.at[source],
            device_id={"seq": owner}, device_id_type=mesh_id,
        )

    def spread(target, owner):
        return pltpu.make_async_remote_copy(
            src_ref=mine, dst_ref=result.at[rows(owner)],
            send_sem=s2.at[target], recv_sem=r2.at[owner],
            device_id={"seq": target}, device_id_type=mesh_id,
        )

    @pl.loop(0, owners)
    def _(owner):
        @pl.when(owner != me)
        def _():
            scatter(owner, me).start()

    tail_copy.start()

    @pl.when(me < owners)
    def _():
        mine[...] = red_ref[rows(lax.rem(me, owners)), :]

        @pl.loop(0, n)
        def _(source):
            @pl.when(source != me)
            def _():
                scatter(lax.rem(me, owners), source).wait_recv()
                mine[...] += parts[source]

        @pl.loop(1, n)
        def _(step):
            spread(lax.rem(me + step, n), lax.rem(me, owners)).start()

        result[rows(lax.rem(me, owners)), :] = mine[...]

    @pl.loop(0, owners)
    def _(owner):
        @pl.when(owner != me)
        def _():
            spread(me, owner).wait_recv()

    total_ref[...] = result[...]
    tail_copy.wait_recv()
    after_ref[...] = jnp.where(me == n - 1, 0.0, tail_in[...])

    @pl.loop(0, owners)
    def _(owner):
        @pl.when(owner != me)
        def _():
            scatter(owner, me).wait_send()

    @pl.when(me < owners)
    def _():
        @pl.loop(1, n)
        def _(step):
            spread(lax.rem(me + step, n), lax.rem(me, owners)).wait_send()

    tail_copy.wait_send()


def per_device(query_raw, key_raw, value_raw, gate_raw, beta_raw, conv_weight, decay_log, grad_out):
    n = lax.axis_size("seq")
    size, channels = gate_raw.shape
    heads = beta_raw.shape[1]
    width = channels // heads
    group = GROUP if heads % GROUP == 0 else 1
    steps = heads // group
    span = group * width
    dlog = decay_log.reshape(1, channels)
    edges = jnp.stack([x[size - PAD :] for x in (query_raw, key_raw, value_raw)])
    halo = lax.ppermute(edges, "seq", [(i, i + 1) for i in range(n - 1)])

    vmem = pl.BlockSpec(memory_space=pltpu.VMEM)
    tokens = pl.BlockSpec((size, span), lambda h: (0, h))
    rows8 = pl.BlockSpec((3, PAD, span), lambda h: (0, 0, h))
    betas = pl.BlockSpec((size, heads), lambda h: (0, 0))
    weights = pl.BlockSpec((3, conv_weight.shape[1], span), lambda h: (0, 0, h))
    single = pl.BlockSpec((1, span), lambda h: (0, h))
    square = pl.BlockSpec((group, width, width), lambda h: (h, 0, 0))
    pairs = pl.BlockSpec((group, size, size), lambda h: (h, 0, 0))
    tall = pl.BlockSpec((group, size, width), lambda h: (h, 0, 0))
    sq = jax.ShapeDtypeStruct((heads, width, width), F32)
    pr = jax.ShapeDtypeStruct((heads, size, size), F32)
    tl = jax.ShapeDtypeStruct((heads, size, width), F32)
    common = (query_raw, key_raw, value_raw, halo, gate_raw, beta_raw, conv_weight, dlog, grad_out)
    common_specs = [
        tokens, tokens, tokens, rows8, tokens, betas, weights, single, tokens,
    ]
    params = pltpu.CompilerParams(vmem_limit_bytes=VMEM_LIMIT)
    trans, offset, adjoint, inv, raw, att, reach = pl.pallas_call(
        functools.partial(maps_kernel, group),
        grid=(steps,),
        out_shape=(sq, sq, sq, pr, pr, pr, tl),
        in_specs=common_specs,
        out_specs=(square, square, square, pairs, pairs, pairs, tall),
        scratch_shapes=[pltpu.VMEM((3 * group, PAD + size, width), F32)],
        compiler_params=params,
        name="maps",
    )(*common)

    buf = pltpu.VMEM((heads, width, width), F32)
    sems = pltpu.SemaphoreType.DMA((heads,))
    state, cotan = pl.pallas_call(
        chain_kernel,
        out_shape=(sq, sq),
        in_specs=[vmem] * 3,
        out_specs=(vmem, vmem),
        scratch_shapes=[buf] * 4 + [sems] * 4,
        compiler_params=pltpu.CompilerParams(
            collective_id=0, has_side_effects=True, vmem_limit_bytes=VMEM_LIMIT
        ),
        name="chain",
    )(trans, offset, adjoint)

    act = jax.ShapeDtypeStruct((size, channels), BF16)
    edge = jax.ShapeDtypeStruct((3, PAD, channels), F32)
    dq, dk, dv, dgate, dbeta, red, tail, last = pl.pallas_call(
        functools.partial(grads_kernel, group),
        grid=(steps,),
        out_shape=(
            act, act, act,
            jax.ShapeDtypeStruct((size, channels), F32),
            jax.ShapeDtypeStruct((size, heads), F32),
            jax.ShapeDtypeStruct((heads * RED, width), F32),
            edge, edge,
        ),
        in_specs=common_specs + [pairs, pairs, pairs, tall, square, square],
        out_specs=(
            tokens, tokens, tokens, tokens, betas,
            pl.BlockSpec((group * RED, width), lambda h: (h, 0)),
            rows8, rows8,
        ),
        scratch_shapes=[
            pltpu.VMEM((3 * group, PAD + size, width), F32),
            pltpu.VMEM((3 * group, PAD + size + PAD, width), F32),
        ],
        compiler_params=params,
        name="grads",
    )(*common, inv, raw, att, reach, state, cotan)

    owners = min(n, heads * RED // 8)
    piece = heads * RED // owners
    total, after = pl.pallas_call(
        finish_kernel,
        out_shape=(jax.ShapeDtypeStruct(red.shape, F32), edge),
        in_specs=[vmem] * 2,
        out_specs=(vmem, vmem),
        scratch_shapes=[
            pltpu.VMEM((n, piece, width), F32),
            pltpu.VMEM((piece, width), F32),
            pltpu.VMEM(red.shape, F32),
            pltpu.VMEM(edge.shape, F32),
            pltpu.SemaphoreType.DMA((owners,)),
            pltpu.SemaphoreType.DMA((n,)),
            pltpu.SemaphoreType.DMA((n,)),
            pltpu.SemaphoreType.DMA((owners,)),
            pltpu.SemaphoreType.DMA,
            pltpu.SemaphoreType.DMA,
        ],
        compiler_params=pltpu.CompilerParams(
            collective_id=1, has_side_effects=True, vmem_limit_bytes=VMEM_LIMIT
        ),
        name="finish",
    )(red, tail)

    ends = (last + after).astype(BF16)
    dq = lax.dynamic_update_slice(dq, ends[0], (size - PAD, 0))
    dk = lax.dynamic_update_slice(dk, ends[1], (size - PAD, 0))
    dv = lax.dynamic_update_slice(dv, ends[2], (size - PAD, 0))
    taps = conv_weight.shape[1]
    total = total.reshape(heads, RED, width)
    conv_sum = total[:, : 3 * taps].transpose(1, 0, 2).reshape(3, taps, channels)
    decay_sum = total[:, 3 * taps].reshape(channels)
    return (dq, dk, dv, dgate, dbeta, conv_sum, decay_sum)


def solution(mesh):
    in_specs = (
        P("seq", "head"),
        P("seq", "head"),
        P("seq", "head"),
        P("seq", "head"),
        P("seq", "head"),
        P(None, None, "head"),
        P("head"),
        P("seq", "head"),
    )
    out_specs = (
        P("seq", "head"),
        P("seq", "head"),
        P("seq", "head"),
        P("seq", "head"),
        P("seq", "head"),
        P(None, None, "head"),
        P("head"),
    )
    return jax.shard_map(
        per_device, mesh=mesh, in_specs=in_specs, out_specs=out_specs, check_vma=False
    )
```

profile of v0, /device:TPU:0, one launch (start us, length us, event | category | flops | bytes accessed | tf_op | source)
XLA Modules:
  0.0 145.2 jit_solution(17664963962097549284)
XLA Ops:
  0.6 0.7 slice_bitcast_fusion.6
  1.4 0.7 slice_bitcast_fusion.4
  2.1 0.0 copy-start.4
  2.1 4.9 %collective-permute-start = (bf16[3,8,1024]{2,1,0:T(8,128)(2,1)S(1)}, bf16[3,8,1024]{2,1,0:T(8,128)(2,1)S(1)}, u32[]{:S(2)}, u32[]{:S(2)}) collective-permute-start(bf16[3,8,1024]{2,1,0:T(8,128)(2,1)S(1)} %pad_maximum_fusion), channel_id=1, source_target_pairs={{0,2},{2,4},{4,6},{6,8},{8,10},{10,12},{12,14},{14,16},{16,18},{18... | collective-permute-start | bytes 147464 | tf_op jit(solution)/shard_map/ppermute | solution.py:482
  7.0 0.0 copy-done.4
  7.0 0.7 copy.16.beta_ref
  7.7 1.0 collective-permute-done.halo_ref
  8.7 0.0 copy-start
  8.7 0.6 copy-done
  9.3 23.4 %maps.1 = (f32[8,128,128]{2,1,0:T(8,128)}, f32[8,128,128]{2,1,0:T(8,128)}, f32[8,128,128]{2,1,0:T(8,128)}, f32[8,128,128]{2,1,0:T(8,128)}, f32[8,128,128]{2,1,0:...) custom-call(bf16[128,1024]{1,0:T(8,128)(2,1)} %q_ref.3, bf16[128,1024]{1,0:T(8,128)(2,1)} %k_ref.3, ...), custom_call_target="tpu_custom_call" | custom-call | tf_op jit(solution)/shard_map/maps/pallas_call | solution.py:501
  32.7 81.7 %chain.1 = (f32[8,128,128]{2,1,0:T(8,128)}, f32[8,128,128]{2,1,0:T(8,128)}) custom-call(f32[8,128,128]{2,1,0:T(8,128)} %get-tuple-element.30.trans_ref, f32[8,128,128]{2,1,0:T(8,128)} %get-tuple-element.31.offset_ref, f32[8,128,128]{2,1,0:T(8,128)} %get-tuple-element.32.adjoint_ref), custom_call_target="tpu_custom_call" | custom-call | tf_op jit(solution)/shard_map/chain/pallas_call | solution.py:514
  114.4 12.6 %grads.1 = (bf16[128,1024]{1,0:T(8,128)(2,1)}, bf16[128,1024]{1,0:T(8,128)(2,1)}, bf16[128,1024]{1,0:T(8,128)(2,1)}, f32[128,1024]{1,0:T(8,128)}, f32[128,8]{1,0...) custom-call(bf16[128,1024]{1,0:T(8,128)(2,1)} %q_ref.3, bf16[128,1024]{1,0:T(8,128)(2,1)} %k_ref.3, ...), custom_call_target="tpu_custom_call" | custom-call | tf_op jit(solution)/shard_map/grads/pallas_call | solution.py:528
  127.0 13.6 %finish.1 = (f32[128,128]{1,0:T(8,128)}, f32[3,8,1024]{2,1,0:T(8,128)}) custom-call(f32[128,128]{1,0:T(8,128)} %get-tuple-element.37.red_ref, f32[3,8,1024]{2,1,0:T(8,128)} %get-tuple-element.38.tail_ref), custom_call_target="tpu_custom_call" | custom-call | tf_op jit(solution)/shard_map/finish/pallas_call | solution.py:554
  140.7 1.4 slice.36
  142.0 0.0 copy-start.3
  142.0 0.9 slice_bitcast_fusion
  142.9 0.0 copy-done.3
  142.9 0.7 copy.18
  143.6 0.0 copy-start.1
  143.6 0.0 copy-start.2
  143.6 0.6 reshape.25
  144.2 0.2 copy-done.1
  144.5 0.1 copy-done.2
  144.5 0.6 fusion
  (3 shorter events, 0.0 us)
Async XLA Ops:
  2.1 4.9 %copy-start.4 = (f32[128,8]{0,1:T(8,128)S(1)}, f32[128,8]{0,1:T(8,128)}, u32[]{:S(2)}) copy-start(f32[128,8]{0,1:T(8,128)} %param.12) | copy-start | bytes 12292
  2.1 6.6 %collective-permute-start = (bf16[3,8,1024]{2,1,0:T(8,128)(2,1)S(1)}, bf16[3,8,1024]{2,1,0:T(8,128)(2,1)S(1)}, u32[]{:S(2)}, u32[]{:S(2)}) collective-permute-start(bf16[3,8,1024]{2,1,0:T(8,128)(2,1)S(1)} %pad_maximum_fusion), channel_id=1, source_target_pairs={{0,2},{2,4},{4,6},{6,8},{8,10},{10,12},{12,14},{14,16},{16,18},{18... | collective-permute-start | bytes 147464 | tf_op jit(solution)/shard_map/ppermute | solution.py:482
  8.7 0.6 copy-start
  142.0 0.9 copy-start.3
  143.6 0.9 copy-start.1
  143.6 1.0 copy-start.2
where the time goes:
time: 146 us; the launch traced here: 145 us
  Pallas kernels  131 us (90%)
  local copies, waits for them, and re-layouts  7.27 us (5%)
  starting transfers between devices  4.87 us (3%)
    pallas_call x1, Pallas kernels, per_device(): pl.pallas_call(chain_kernel, out_shape=(sq, sq), in_specs=[vmem] * 3, out...  81.7 us
    pallas_call x1, Pallas kernels, per_device(): pl.pallas_call(functools.partial(maps_kernel, group), grid=(steps,), out_...  23.4 us
    pallas_call x1, Pallas kernels, per_device(): pl.pallas_call(finish_kernel, out_shape=(jax.ShapeDtypeStruct(red.shape,...  13.6 us
    pallas_call x1, Pallas kernels, per_device(): pl.pallas_call(functools.partial(grads_kernel, group), grid=(steps,), out...  12.6 us
    ppermute x1, starting transfers between devices, per_device(): halo = lax.ppermute(edges, 'seq', [(i, i + 1) for i in range(n - 1)])  4.87 us
  transfers between devices with their start and end apart: 1, of which 1 were waited for; matrix products, arithmetic and copies ran while one was open for 0% of the time, Pallas kernels for 0%

commit v1 on v0

--- a/solution.py
+++ b/solution.py
@@ -1,4 +1,5 @@
 import functools
+import math
 
 import jax
 import jax.numpy as jnp
@@ -12,7 +13,8 @@
 EPS = 1e-06
 PAD = 8
 RED = 16
-GROUP = 2
+GROUP = 4
+TEAM = 4
 VMEM_LIMIT = 60 * 1024 * 1024
 
 
@@ -124,20 +126,22 @@
     )
 
 
-def unit_inverse(a):
-    size = a.shape[0]
+def unit_inverses(coups):
+    size = coups[0].shape[0]
     r, c = iotas(size)
     ident = jnp.where(r == c, 1.0, 0.0)
     shift = 3
-    small = jnp.where((r >> shift) == (c >> shift), a, 0.0)
-    p2 = mm(small, small)
-    base = ident - small
-    base = base + mm(base, p2)
-    p4 = mm(p2, p2)
-    d = base + mm(base, p4)
+    inside = (r >> shift) == (c >> shift)
+    small = [jnp.where(inside, a, 0.0) for a in coups]
+    p2 = [mm(a, a) for a in small]
+    base = [ident - a for a in small]
+    p4 = [mm(p, p) for p in p2]
+    base = [x + mm(x, p) for x, p in zip(base, p2)]
+    d = [x + mm(x, p) for x, p in zip(base, p4)]
     while (1 << shift) < size:
         joined = ((r >> (shift + 1)) == (c >> (shift + 1))) & ((r >> shift) != (c >> shift))
-        d = d - mm(d, mm(jnp.where(joined, a, 0.0), d))
+        low = [mm(jnp.where(joined, a, 0.0), x) for a, x in zip(coups, d)]
+        d = [x - mm(x, y) for x, y in zip(d, low)]
         shift += 1
     return d
 
@@ -151,6 +155,7 @@
     size = q_ref.shape[0]
     width = trans_ref.shape[1]
     r, c = iotas(size)
+    held = []
     for g in range(group):
         cols = slice(g * width, (g + 1) * width)
         head = pl.program_id(0) * group + g
@@ -170,107 +175,194 @@
         att, raw = pair_scores(qk_up, k * down, qk_cross, kc)
         att = jnp.where(r >= c, att, 0.0)
         raw = jnp.where(r > c, raw, 0.0)
-        inv = unit_inverse(raw * beta)
-        by = mm(inv, jnp.concatenate([beta * k * full, beta * v], 1))
-        by_k = by[:, :width]
-        ends = mm(k * end, by, ta=True)
-        rr, cc = iotas(width)
-        trans_ref[g] = jnp.where(rr == cc, dend, 0.0) - ends[:, :width]
-        offset_ref[g] = ends[:, width:]
-        grad = grad_ref[:, cols].astype(F32)
-        reach = mm(att, grad, ta=True)
-        adjoint_ref[g] = mm(
-            jnp.concatenate([q * full, -by_k], 0), jnp.concatenate([grad, reach], 0), ta=True
-        )
-        inv_ref[g] = inv
         raw_ref[g] = raw
         att_ref[g] = att
-        reach_ref[g] = reach
+        reach_ref[g] = mm(att, grad_ref[:, cols].astype(F32), ta=True)
+        inputs = jnp.concatenate([beta * k * full, beta * v], 1)
+        held.append((raw * beta, inputs, k * end, dend, q * full))
+    invs = unit_inverses([item[0] for item in held])
+    bys = [mm(inv, item[1]) for inv, item in zip(invs, held)]
+    rr, cc = iotas(width)
+    for g in range(group):
+        cols = slice(g * width, (g + 1) * width)
+        inv_ref[g] = invs[g]
+        ends = mm(held[g][2], bys[g], ta=True)
+        trans_ref[g] = jnp.where(rr == cc, held[g][3], 0.0) - ends[:, :width]
+        offset_ref[g] = ends[:, width:]
+        adjoint_ref[g] = mm(
+            jnp.concatenate([held[g][4], -bys[g][:, :width]], 0),
+            jnp.concatenate([grad_ref[:, cols].astype(F32), reach_ref[g]], 0),
+            ta=True,
+        )
 
 
 def chain_kernel(
     trans_ref, offset_ref, adjoint_ref, state_ref, cotan_ref,
-    send_s, recv_s, send_g, recv_g, ss, rs, sg, rg,
+    gt, gb, ga, pre_t, pre_b, send_s, send_g, in_s, in_g, out_s, out_g, back_s, back_g,
+    at_s, at_r, ab_s, ab_r, aa_s, aa_r, ss, rs, sg, rg, bs_s, bs_r, bg_s, bg_r,
 ):
     n = lax.axis_size("seq")
     me = lax.axis_index("seq")
-    right = lax.rem(me + 1, n)
-    left = lax.rem(me + n - 1, n)
-    heads = trans_ref.shape[0]
+    team, mine_heads = gt.shape[0], gt.shape[1]
+    mine = lax.rem(me, team)
+    base = me - mine
+    level = me // team
+    levels = n // team
+    mesh_id = pl.DeviceIdType.MESH
+    after = lax.rem(me + team, n)
+    ahead = lax.rem(me + n - team, n)
     barrier = pltpu.get_barrier_semaphore()
-    for peer in (left, right):
-        pl.semaphore_signal(
-            barrier, inc=1, device_id={"seq": peer}, device_id_type=pl.DeviceIdType.MESH
-        )
-    pl.semaphore_wait(barrier, 2)
+    peers = [base + lax.rem(mine + i, team) for i in range(1, team)]
+    links = peers + ([after, ahead] if levels > 1 else [])
+    for peer in links:
+        pl.semaphore_signal(barrier, inc=1, device_id={"seq": peer}, device_id_type=mesh_id)
+    pl.semaphore_wait(barrier, len(links))
+
+    def block(member):
+        return pl.ds(member * mine_heads, mine_heads)
+
+    def spread(source, target, ref, dst, send, recv):
+        return pltpu.make_async_remote_copy(
+            src_ref=ref.at[block(target)], dst_ref=dst.at[source],
+            send_sem=send.at[target], recv_sem=recv.at[source],
+            device_id={"seq": base + target}, device_id_type=mesh_id,
+        )
+
+    kinds = (
+        (trans_ref, gt, at_s, at_r), (offset_ref, gb, ab_s, ab_r), (adjoint_ref, ga, aa_s, aa_r)
+    )
+    others = [lax.rem(mine + i, team) for i in range(1, team)]
+    for kind in kinds:
+        for other in others:
+            spread(mine, other, *kind).start()
+    for ref, dst, _, _ in kinds:
+        dst[mine] = ref[block(mine)]
+    for kind in kinds[:2]:
+        for other in others:
+            spread(other, other, *kind).wait_recv()
+
+    for h in range(mine_heads):
+        pre_t[0, h] = gt[0, h]
+        pre_b[0, h] = gb[0, h]
+    for j in range(1, team):
+        for h in range(mine_heads):
+            both = mm(gt[j, h], jnp.concatenate([pre_t[j - 1, h], pre_b[j - 1, h]], 1))
+            width = both.shape[1] // 2
+            pre_t[j, h] = both[:, :width]
+            pre_b[j, h] = both[:, width:] + gb[j, h]
+    for other in others:
+        spread(other, other, *kinds[2]).wait_recv()
+    for h in range(mine_heads):
+        send_g[h] = ga[team - 1, h]
+    for j in range(team - 2, -1, -1):
+        for h in range(mine_heads):
+            send_g[h] = mm(gt[j, h], send_g[h], ta=True) + ga[j, h]
 
     def state_copy(h):
         return pltpu.make_async_remote_copy(
-            src_ref=send_s.at[h], dst_ref=recv_s.at[h], send_sem=ss.at[h], recv_sem=rs.at[h],
-            device_id={"seq": right}, device_id_type=pl.DeviceIdType.MESH,
+            src_ref=send_s.at[h], dst_ref=in_s.at[h], send_sem=ss.at[h], recv_sem=rs.at[h],
+            device_id={"seq": after}, device_id_type=mesh_id,
         )
 
     def cotan_copy(h):
         return pltpu.make_async_remote_copy(
-            src_ref=send_g.at[h], dst_ref=recv_g.at[h], send_sem=sg.at[h], recv_sem=rg.at[h],
-            device_id={"seq": left}, device_id_type=pl.DeviceIdType.MESH,
-        )
+            src_ref=send_g.at[h], dst_ref=in_g.at[h], send_sem=sg.at[h], recv_sem=rg.at[h],
+            device_id={"seq": ahead}, device_id_type=mesh_id,
+        )
+
+    def give(member, owner, src, dst, send, recv):
+        return pltpu.make_async_remote_copy(
+            src_ref=src.at[member], dst_ref=dst.at[block(owner)],
+            send_sem=send.at[member], recv_sem=recv.at[owner],
+            device_id={"seq": base + member}, device_id_type=mesh_id,
+        )
+
+    states = (out_s, back_s, bs_s, bs_r)
+    cotans = (out_g, back_g, bg_s, bg_r)
 
     def forward():
-        @pl.loop(0, heads)
-        def _(h):
-            @pl.when(me == 0)
+        for h in range(mine_heads):
+            @pl.when(level == 0)
             def _():
-                state_ref[h] = jnp.zeros_like(state_ref[h])
-                send_s[h] = offset_ref[h]
-
-            @pl.when(me > 0)
+                out_s[0, h] = jnp.zeros_like(out_s[0, h])
+                send_s[h] = pre_b[team - 1, h]
+
+            @pl.when(level > 0)
             def _():
                 state_copy(h).wait_recv()
-                state = recv_s[h]
-                state_ref[h] = state
-                send_s[h] = mm(trans_ref[h], state) + offset_ref[h]
-
-            @pl.when(me < n - 1)
+                state = in_s[h]
+                out_s[0, h] = state
+
+                @pl.when(level < levels - 1)
+                def _():
+                    send_s[h] = mm(pre_t[team - 1, h], state) + pre_b[team - 1, h]
+
+            @pl.when(level < levels - 1)
             def _():
                 state_copy(h).start()
 
+        for j in range(1, team):
+            for h in range(mine_heads):
+                out_s[j, h] = mm(pre_t[j - 1, h], out_s[0, h]) + pre_b[j - 1, h]
+        for other in others:
+            give(other, mine, *states).start()
+
     def backward():
-        @pl.loop(0, heads)
-        def _(h):
-            @pl.when(me == n - 1)
+        for h in range(mine_heads):
+            @pl.when(level == levels - 1)
             def _():
-                cotan_ref[h] = jnp.zeros_like(cotan_ref[h])
-                send_g[h] = adjoint_ref[h]
-
-            @pl.when(me < n - 1)
+                out_g[team - 1, h] = jnp.zeros_like(out_g[0, h])
+
+            @pl.when(level < levels - 1)
             def _():
                 cotan_copy(h).wait_recv()
-                cotan = recv_g[h]
-                cotan_ref[h] = cotan
-                send_g[h] = mm(trans_ref[h], cotan, ta=True) + adjoint_ref[h]
-
-            @pl.when(me > 0)
+                cotan = in_g[h]
+                out_g[team - 1, h] = cotan
+
+                @pl.when(level > 0)
+                def _():
+                    send_g[h] = mm(pre_t[team - 1, h], cotan, ta=True) + send_g[h]
+
+            @pl.when(level > 0)
             def _():
                 cotan_copy(h).start()
 
-    @pl.when(me < n // 2)
+        for j in range(team - 1, 0, -1):
+            for h in range(mine_heads):
+                out_g[j - 1, h] = mm(gt[j, h], out_g[j, h], ta=True) + ga[j, h]
+
+        for other in others:
+            give(other, mine, *cotans).start()
+
+    @pl.when(level < levels // 2)
     def _():
         forward()
         backward()
 
-    @pl.when(me >= n // 2)
+    @pl.when(level >= levels // 2)
     def _():
         backward()
         forward()
 
-    @pl.loop(0, heads)
-    def _(h):
-        @pl.when(me < n - 1)
+    back_s[block(mine)] = out_s[mine]
+    back_g[block(mine)] = out_g[mine]
+    for other in others:
+        give(mine, other, *states).wait_recv()
+    for other in others:
+        give(mine, other, *cotans).wait_recv()
+    state_ref[...] = back_s[...]
+    cotan_ref[...] = back_g[...]
+    for other in others:
+        for kind in kinds:
+            spread(mine, other, *kind).wait_send()
+        give(other, mine, *states).wait_send()
+        give(other, mine, *cotans).wait_send()
+    for h in range(mine_heads):
+        @pl.when(level < levels - 1)
         def _():
             state_copy(h).wait_send()
 
-        @pl.when(me > 0)
+        @pl.when(level > 0)
         def _():
             cotan_copy(h).wait_send()
 
@@ -377,7 +469,7 @@
 
 
 def finish_kernel(
-    red_ref, tail_ref, total_ref, after_ref,
+    red_ref, tail_ref, conv_ref, decay_ref, after_ref,
     parts, mine, result, tail_in, s1, r1, s2, r2, st, rt,
 ):
     n = lax.axis_size("seq")
@@ -450,7 +542,15 @@
         def _():
             spread(me, owner).wait_recv()
 
-    total_ref[...] = result[...]
+    width = result.shape[1]
+    taps = conv_ref.shape[1]
+    for h in range(result.shape[0] // RED):
+        cols = slice(h * width, (h + 1) * width)
+        for j in range(3):
+            start = h * RED + j * taps
+            conv_ref[j, :, cols] = result[start : start + taps, :]
+        start = h * RED + 3 * taps
+        decay_ref[:, cols] = result[start : start + 1, :]
     tail_copy.wait_recv()
     after_ref[...] = jnp.where(me == n - 1, 0.0, tail_in[...])
 
@@ -509,14 +609,20 @@
         name="maps",
     )(*common)
 
-    buf = pltpu.VMEM((heads, width, width), F32)
-    sems = pltpu.SemaphoreType.DMA((heads,))
+    team = math.gcd(TEAM, math.gcd(n, heads))
+    part = heads // team
+    whole = pltpu.VMEM((heads, width, width), F32)
+    few = pltpu.VMEM((part, width, width), F32)
+    many = pltpu.VMEM((team, part, width, width), F32)
+    sems = pltpu.SemaphoreType.DMA((team,))
+    hops = pltpu.SemaphoreType.DMA((part,))
     state, cotan = pl.pallas_call(
         chain_kernel,
         out_shape=(sq, sq),
         in_specs=[vmem] * 3,
         out_specs=(vmem, vmem),
-        scratch_shapes=[buf] * 4 + [sems] * 4,
+        scratch_shapes=[many] * 5 + [few] * 4 + [many] * 2 + [whole] * 2
+        + [sems] * 6 + [hops] * 4 + [sems] * 4,
         compiler_params=pltpu.CompilerParams(
             collective_id=0, has_side_effects=True, vmem_limit_bytes=VMEM_LIMIT
         ),
@@ -551,11 +657,15 @@
 
     owners = min(n, heads * RED // 8)
     piece = heads * RED // owners
-    total, after = pl.pallas_call(
+    conv_sum, decay_sum, after = pl.pallas_call(
         finish_kernel,
-        out_shape=(jax.ShapeDtypeStruct(red.shape, F32), edge),
+        out_shape=(
+            jax.ShapeDtypeStruct(conv_weight.shape, F32),
+            jax.ShapeDtypeStruct((1, channels), F32),
+            edge,
+        ),
         in_specs=[vmem] * 2,
-        out_specs=(vmem, vmem),
+        out_specs=(vmem, vmem, vmem),
         scratch_shapes=[
             pltpu.VMEM((n, piece, width), F32),
             pltpu.VMEM((piece, width), F32),
@@ -578,11 +688,7 @@
     dq = lax.dynamic_update_slice(dq, ends[0], (size - PAD, 0))
     dk = lax.dynamic_update_slice(dk, ends[1], (size - PAD, 0))
     dv = lax.dynamic_update_slice(dv, ends[2], (size - PAD, 0))
-    taps = conv_weight.shape[1]
-    total = total.reshape(heads, RED, width)
-    conv_sum = total[:, : 3 * taps].transpose(1, 0, 2).reshape(3, taps, channels)
-    decay_sum = total[:, 3 * taps].reshape(channels)
-    return (dq, dk, dv, dgate, dbeta, conv_sum, decay_sum)
+    return (dq, dk, dv, dgate, dbeta, conv_sum, decay_sum.reshape(channels))
 
 
 def solution(mesh):

time: 146 us -> 96.9 us (0.66)
  Pallas kernels: 131 us -> 82.5 us
    pallas_call x1, Pallas kernels: 81.7 us -> 43.4 us  [per_device(): pl.pallas_call(chain_kernel, out_shape=(sq, sq), in_specs=[vmem] * 3, out...]
    pallas_call x1, Pallas kernels: 23.4 us -> 11.6 us  [per_device(): pl.pallas_call(functools.partial(maps_kernel, group), grid=(steps,), out_...]
    unnamed x12 -> x14, local copies, waits for them, and re-layouts: 2.3 us -> 4.28 us
  transfers between devices with their start and end apart: 1 -> 1, of which waited for: 1 -> 1; matrix products, arithmetic and copies ran while one was open for 0% -> 1% of each run, Pallas kernels for 0% -> 0%
where the time goes in v1:
time: 96.9 us; the launch traced here: 96.4 us
  Pallas kernels  82.5 us (85%)
  local copies, waits for them, and re-layouts  6.37 us (7%)
  starting transfers between devices  4.87 us (5%)
  waiting for transfers between devices  1 us (1%)
    pallas_call x1, Pallas kernels, per_device(): pl.pallas_call(chain_kernel, out_shape=(sq, sq), in_specs=[vmem] * 3, out...  43.4 us
    pallas_call x1, Pallas kernels, per_device(): pl.pallas_call(finish_kernel, out_shape=(jax.ShapeDtypeStruct(conv_weight...  14.8 us
    pallas_call x1, Pallas kernels, per_device(): pl.pallas_call(functools.partial(grads_kernel, group), grid=(steps,), out...  12.7 us
    pallas_call x1, Pallas kernels, per_device(): pl.pallas_call(functools.partial(maps_kernel, group), grid=(steps,), out_...  11.6 us
    ppermute x1, starting transfers between devices, per_device(): halo = lax.ppermute(edges, 'seq', [(i, i + 1) for i in range(n - 1)])  4.87 us
    unnamed x14, local copies, waits for them, and re-layouts  4.28 us
  transfers between devices with their start and end apart: 1, of which 1 were waited for; matrix products, arithmetic and copies ran while one was open for 1% of the time, Pallas kernels for 0%

profile of v1, /device:TPU:0, one launch (start us, length us, event | category | flops | bytes accessed | tf_op | source)
XLA Modules:
  0.0 96.4 jit_solution(13613764935710012785)
XLA Ops:
  0.6 0.7 slice_bitcast_fusion.5
  1.4 0.7 slice_bitcast_fusion.3
  2.1 0.0 copy-start.3
  2.1 4.9 %collective-permute-start = (bf16[3,8,1024]{2,1,0:T(8,128)(2,1)S(1)}, bf16[3,8,1024]{2,1,0:T(8,128)(2,1)S(1)}, u32[]{:S(2)}, u32[]{:S(2)}) collective-permute-start(bf16[3,8,1024]{2,1,0:T(8,128)(2,1)S(1)} %pad_maximum_fusion), channel_id=1, source_target_pairs={{0,2},{2,4},{4,6},{6,8},{8,10},{10,12},{12,14},{14,16},{16,18},{18... | collective-permute-start | bytes 147464 | tf_op jit(solution)/shard_map/ppermute | solution.py:582
  7.0 0.0 copy-done.3
  7.0 0.7 copy.16.beta_ref
  7.7 1.0 %collective-permute-done.halo_ref = bf16[3,8,1024]{2,1,0:T(8,128)(2,1)S(1)} collective-permute-done((bf16[3,8,1024]{2,1,0:T(8,128)(2,1)S(1)}, bf16[3,8,1024]{2,1,0:T(8,128)(2,1)S(1)}, u32[]{:S(2)}, u32[]{:S(2)}) %collective-permute-start) | collective-permute-done | bytes 49184 | tf_op jit(solution)/shard_map/ppermute | solution.py:582
  8.7 0.0 copy-start
  8.7 0.6 copy-done
  9.3 11.6 %maps.1 = (f32[8,128,128]{2,1,0:T(8,128)}, f32[8,128,128]{2,1,0:T(8,128)}, f32[8,128,128]{2,1,0:T(8,128)}, f32[8,128,128]{2,1,0:T(8,128)}, f32[8,128,128]{2,1,0:...) custom-call(bf16[128,1024]{1,0:T(8,128)(2,1)} %q_ref.3, bf16[128,1024]{1,0:T(8,128)(2,1)} %k_ref.3, ...), custom_call_target="tpu_custom_call" | custom-call | tf_op jit(solution)/shard_map/maps/pallas_call | solution.py:601
  21.0 43.4 %chain.1 = (f32[8,128,128]{2,1,0:T(8,128)}, f32[8,128,128]{2,1,0:T(8,128)}) custom-call(f32[8,128,128]{2,1,0:T(8,128)} %get-tuple-element.31.trans_ref, f32[8,128,128]{2,1,0:T(8,128)} %get-tuple-element.32.offset_ref, f32[8,128,128]{2,1,0:T(8,128)} %get-tuple-element.33.adjoint_ref), custom_call_target="tpu_custom_call" | custom-call | tf_op jit(solution)/shard_map/chain/pallas_call | solution.py:619
  64.3 12.7 %grads.1 = (bf16[128,1024]{1,0:T(8,128)(2,1)}, bf16[128,1024]{1,0:T(8,128)(2,1)}, bf16[128,1024]{1,0:T(8,128)(2,1)}, f32[128,1024]{1,0:T(8,128)}, f32[128,8]{1,0...) custom-call(bf16[128,1024]{1,0:T(8,128)(2,1)} %q_ref.3, bf16[128,1024]{1,0:T(8,128)(2,1)} %k_ref.3, ...), custom_call_target="tpu_custom_call" | custom-call | tf_op jit(solution)/shard_map/grads/pallas_call | solution.py:634
  77.1 1.5 %copy.17 = f32[128,8]{0,1:T(8,128)} copy(f32[128,8]{1,0:T(8,128)} %get-tuple-element.51) | data formatting | bytes 8192
  78.6 0.0 copy-start.1
  78.6 14.8 %finish.1 = (f32[3,4,1024]{2,1,0:T(4,128)}, f32[1,1024]{1,0:T(1,128)}, f32[3,8,1024]{2,1,0:T(8,128)}) custom-call(f32[128,128]{1,0:T(8,128)} %get-tuple-element.38.red_ref, f32[3,8,1024]{2,1,0:T(8,128)} %get-tuple-element.39.tail_ref), custom_call_target="tpu_custom_call" | custom-call | tf_op jit(solution)/shard_map/finish/pallas_call | solution.py:660
  93.4 0.0 copy-done.1
  93.4 0.9 add_convert_fusion
  94.3 0.0 copy-start.2
  94.3 0.6 fusion
  94.9 0.2 copy-done.2
  95.1 0.0 copy-start.4
  95.1 0.6 copy.23
  95.7 0.1 copy-done.4
  95.8 0.6 copy.24
  (1 shorter events, 0.0 us)
Async XLA Ops:
  2.1 4.9 %copy-start.3 = (f32[128,8]{0,1:T(8,128)S(1)}, f32[128,8]{0,1:T(8,128)}, u32[]{:S(2)}) copy-start(f32[128,8]{0,1:T(8,128)} %param.12) | copy-start | bytes 12292
  2.1 6.6 %collective-permute-start = (bf16[3,8,1024]{2,1,0:T(8,128)(2,1)S(1)}, bf16[3,8,1024]{2,1,0:T(8,128)(2,1)S(1)}, u32[]{:S(2)}, u32[]{:S(2)}) collective-permute-start(bf16[3,8,1024]{2,1,0:T(8,128)(2,1)S(1)} %pad_maximum_fusion), channel_id=1, source_target_pairs={{0,2},{2,4},{4,6},{6,8},{8,10},{10,12},{12,14},{14,16},{16,18},{18... | collective-permute-start | bytes 147464 | tf_op jit(solution)/shard_map/ppermute | solution.py:582
  8.7 0.6 copy-start
  78.6 14.8 %copy-start.1 = (f32[3,8,1024]{2,1,0:T(8,128)S(1)}, f32[3,8,1024]{2,1,0:T(8,128)}, u32[]{:S(2)}) copy-start(f32[3,8,1024]{2,1,0:T(8,128)} %get-tuple-element.37) | copy-start | bytes 294916
  94.3 0.8 copy-start.2
  95.1 0.7 copy-start.4

commit v2 on v1

--- a/solution.py
+++ b/solution.py
@@ -14,6 +14,8 @@
 PAD = 8
 RED = 16
 GROUP = 4
+GROUP_MAPS = 4
+LINK = F32
 TEAM = 4
 VMEM_LIMIT = 60 * 1024 * 1024
 
@@ -146,60 +148,13 @@
     return d
 
 
-def maps_kernel(
+def scan_kernel(
     group,
-    q_ref, k_ref, v_ref, halo_ref, gate_ref, beta_ref, w_ref, dlog_ref, grad_ref,
-    trans_ref, offset_ref, adjoint_ref, inv_ref, raw_ref, att_ref, reach_ref,
-    ext,
-):
-    size = q_ref.shape[0]
-    width = trans_ref.shape[1]
-    r, c = iotas(size)
-    held = []
-    for g in range(group):
-        cols = slice(g * width, (g + 1) * width)
-        head = pl.program_id(0) * group + g
-        pre_q, _ = conv_pre(ext.at[3 * g], q_ref, halo_ref, w_ref, 0, cols)
-        pre_k, _ = conv_pre(ext.at[3 * g + 1], k_ref, halo_ref, w_ref, 1, cols)
-        pre_v, _ = conv_pre(ext.at[3 * g + 2], v_ref, halo_ref, w_ref, 2, cols)
-        q, _ = unit(pre_q * sigmoid(pre_q))
-        k, _ = unit(pre_k * sigmoid(pre_k))
-        v = pre_v * sigmoid(pre_v)
-        beta = sigmoid(pick_column(beta_ref, head))
-        ld, speed, up, down, cross, full, end, dend, first = decays(
-            gate_ref[:, cols], dlog_ref[:, cols]
-        )
-        kc = k * cross
-        qk_up = jnp.concatenate([q * up, k * up], 0)
-        qk_cross = jnp.concatenate([q * cross, kc], 0)
-        att, raw = pair_scores(qk_up, k * down, qk_cross, kc)
-        att = jnp.where(r >= c, att, 0.0)
-        raw = jnp.where(r > c, raw, 0.0)
-        raw_ref[g] = raw
-        att_ref[g] = att
-        reach_ref[g] = mm(att, grad_ref[:, cols].astype(F32), ta=True)
-        inputs = jnp.concatenate([beta * k * full, beta * v], 1)
-        held.append((raw * beta, inputs, k * end, dend, q * full))
-    invs = unit_inverses([item[0] for item in held])
-    bys = [mm(inv, item[1]) for inv, item in zip(invs, held)]
-    rr, cc = iotas(width)
-    for g in range(group):
-        cols = slice(g * width, (g + 1) * width)
-        inv_ref[g] = invs[g]
-        ends = mm(held[g][2], bys[g], ta=True)
-        trans_ref[g] = jnp.where(rr == cc, held[g][3], 0.0) - ends[:, :width]
-        offset_ref[g] = ends[:, width:]
-        adjoint_ref[g] = mm(
-            jnp.concatenate([held[g][4], -bys[g][:, :width]], 0),
-            jnp.concatenate([grad_ref[:, cols].astype(F32), reach_ref[g]], 0),
-            ta=True,
-        )
-
-
-def chain_kernel(
-    trans_ref, offset_ref, adjoint_ref, state_ref, cotan_ref,
+    q_ref, k_ref, v_ref, gate_ref, beta_ref, w_ref, dlog_ref, grad_ref,
+    halo_ref, inv_ref, raw_ref, att_ref, reach_ref, state_ref, cotan_ref,
+    ext, halo_in, trans, offset, adjoint,
     gt, gb, ga, pre_t, pre_b, send_s, send_g, in_s, in_g, out_s, out_g, back_s, back_g,
-    at_s, at_r, ab_s, ab_r, aa_s, aa_r, ss, rs, sg, rg, bs_s, bs_r, bg_s, bg_r,
+    hs, hr, at_s, at_r, ab_s, ab_r, aa_s, aa_r, ss, rs, sg, rg, bs_s, bs_r, bg_s, bg_r,
 ):
     n = lax.axis_size("seq")
     me = lax.axis_index("seq")
@@ -209,14 +164,31 @@
     level = me // team
     levels = n // team
     mesh_id = pl.DeviceIdType.MESH
+    right = lax.rem(me + 1, n)
+    left = lax.rem(me + n - 1, n)
     after = lax.rem(me + team, n)
     ahead = lax.rem(me + n - team, n)
     barrier = pltpu.get_barrier_semaphore()
     peers = [base + lax.rem(mine + i, team) for i in range(1, team)]
-    links = peers + ([after, ahead] if levels > 1 else [])
+    links = peers + [right, left] + ([after, ahead] if levels > 1 else [])
     for peer in links:
         pl.semaphore_signal(barrier, inc=1, device_id={"seq": peer}, device_id_type=mesh_id)
     pl.semaphore_wait(barrier, len(links))
+
+    size = q_ref.shape[0]
+    heads, width = trans.shape[0], trans.shape[1]
+
+    def halo_copy(j, ref):
+        return pltpu.make_async_remote_copy(
+            src_ref=ref.at[pl.ds(size - PAD, PAD)], dst_ref=halo_in.at[j],
+            send_sem=hs.at[j], recv_sem=hr.at[j],
+            device_id={"seq": right}, device_id_type=mesh_id,
+        )
+
+    @pl.when(me < n - 1)
+    def _():
+        for j, ref in enumerate((q_ref, k_ref, v_ref)):
+            halo_copy(j, ref).start()
 
     def block(member):
         return pl.ds(member * mine_heads, mine_heads)
@@ -229,12 +201,67 @@
         )
 
     kinds = (
-        (trans_ref, gt, at_s, at_r), (offset_ref, gb, ab_s, ab_r), (adjoint_ref, ga, aa_s, aa_r)
+        (trans, gt, at_s, at_r), (offset, gb, ab_s, ab_r), (adjoint, ga, aa_s, aa_r)
     )
     others = [lax.rem(mine + i, team) for i in range(1, team)]
-    for kind in kinds:
-        for other in others:
-            spread(mine, other, *kind).start()
+    order = others + [mine]
+    r, c = iotas(size)
+    rr, cc = iotas(width)
+    for begin in range(0, heads, group):
+        held = []
+        places = []
+        for g in range(group):
+            at = begin + g
+            head = order[at // mine_heads] * mine_heads + at % mine_heads
+            places.append((head, pl.ds(pl.multiple_of(head * width, width), width)))
+        fades = [decays(gate_ref[:, cols], dlog_ref[:, cols]) for _, cols in places]
+        if begin == 0:
+            @pl.when(me == 0)
+            def _():
+                halo_in[...] = jnp.zeros_like(halo_in)
+
+            @pl.when(me > 0)
+            def _():
+                for j, ref in enumerate((q_ref, k_ref, v_ref)):
+                    halo_copy(j, ref).wait_recv()
+
+            halo_ref[...] = halo_in[...]
+        for g, (head, cols) in enumerate(places):
+            pre_q, _ = conv_pre(ext.at[3 * g], q_ref, halo_in, w_ref, 0, cols)
+            pre_k, _ = conv_pre(ext.at[3 * g + 1], k_ref, halo_in, w_ref, 1, cols)
+            pre_v, _ = conv_pre(ext.at[3 * g + 2], v_ref, halo_in, w_ref, 2, cols)
+            q, _ = unit(pre_q * sigmoid(pre_q))
+            k, _ = unit(pre_k * sigmoid(pre_k))
+            v = pre_v * sigmoid(pre_v)
+            beta = sigmoid(pick_column(beta_ref, head))
+            ld, speed, up, down, cross, full, end, dend, first = fades[g]
+            kc = k * cross
+            qk_up = jnp.concatenate([q * up, k * up], 0)
+            qk_cross = jnp.concatenate([q * cross, kc], 0)
+            att, raw = pair_scores(qk_up, k * down, qk_cross, kc)
+            att = jnp.where(r >= c, att, 0.0)
+            raw = jnp.where(r > c, raw, 0.0)
+            raw_ref[head] = raw
+            att_ref[head] = att
+            reach_ref[head] = mm(att, grad_ref[:, cols].astype(F32), ta=True)
+            inputs = jnp.concatenate([beta * k * full, beta * v], 1)
+            held.append((raw * beta, inputs, k * end, dend, q * full))
+        invs = unit_inverses([item[0] for item in held])
+        bys = [mm(inv, item[1]) for inv, item in zip(invs, held)]
+        for g, (head, cols) in enumerate(places):
+            inv_ref[head] = invs[g]
+            ends = mm(held[g][2], bys[g], ta=True)
+            trans[head] = (jnp.where(rr == cc, held[g][3], 0.0) - ends[:, :width]).astype(LINK)
+            offset[head] = ends[:, width:].astype(LINK)
+            adjoint[head] = mm(
+                jnp.concatenate([held[g][4], -bys[g][:, :width]], 0),
+                jnp.concatenate([grad_ref[:, cols].astype(F32), reach_ref[head]], 0),
+                ta=True,
+            ).astype(LINK)
+        for i in range(begin // mine_heads, (begin + group) // mine_heads):
+            if i < len(others):
+                for kind in kinds:
+                    spread(mine, others[i], *kind).start()
     for ref, dst, _, _ in kinds:
         dst[mine] = ref[block(mine)]
     for kind in kinds[:2]:
@@ -242,21 +269,20 @@
             spread(other, other, *kind).wait_recv()
 
     for h in range(mine_heads):
-        pre_t[0, h] = gt[0, h]
-        pre_b[0, h] = gb[0, h]
+        pre_t[0, h] = gt[0, h].astype(F32)
+        pre_b[0, h] = gb[0, h].astype(F32)
     for j in range(1, team):
         for h in range(mine_heads):
-            both = mm(gt[j, h], jnp.concatenate([pre_t[j - 1, h], pre_b[j - 1, h]], 1))
-            width = both.shape[1] // 2
+            both = mm(gt[j, h].astype(F32), jnp.concatenate([pre_t[j - 1, h], pre_b[j - 1, h]], 1))
             pre_t[j, h] = both[:, :width]
-            pre_b[j, h] = both[:, width:] + gb[j, h]
+            pre_b[j, h] = both[:, width:] + gb[j, h].astype(F32)
     for other in others:
         spread(other, other, *kinds[2]).wait_recv()
     for h in range(mine_heads):
-        send_g[h] = ga[team - 1, h]
+        send_g[h] = ga[team - 1, h].astype(F32)
     for j in range(team - 2, -1, -1):
         for h in range(mine_heads):
-            send_g[h] = mm(gt[j, h], send_g[h], ta=True) + ga[j, h]
+            send_g[h] = mm(gt[j, h].astype(F32), send_g[h], ta=True) + ga[j, h].astype(F32)
 
     def state_copy(h):
         return pltpu.make_async_remote_copy(
@@ -284,14 +310,13 @@
         for h in range(mine_heads):
             @pl.when(level == 0)
             def _():
-                out_s[0, h] = jnp.zeros_like(out_s[0, h])
+                in_s[h] = jnp.zeros_like(in_s[h])
                 send_s[h] = pre_b[team - 1, h]
 
             @pl.when(level > 0)
             def _():
                 state_copy(h).wait_recv()
                 state = in_s[h]
-                out_s[0, h] = state
 
                 @pl.when(level < levels - 1)
                 def _():
@@ -301,9 +326,11 @@
             def _():
                 state_copy(h).start()
 
-        for j in range(1, team):
-            for h in range(mine_heads):
-                out_s[j, h] = mm(pre_t[j - 1, h], out_s[0, h]) + pre_b[j - 1, h]
+        for h in range(mine_heads):
+            state = in_s[h]
+            out_s[0, h] = state.astype(LINK)
+            for j in range(1, team):
+                out_s[j, h] = (mm(pre_t[j - 1, h], state) + pre_b[j - 1, h]).astype(LINK)
         for other in others:
             give(other, mine, *states).start()
 
@@ -311,13 +338,12 @@
         for h in range(mine_heads):
             @pl.when(level == levels - 1)
             def _():
-                out_g[team - 1, h] = jnp.zeros_like(out_g[0, h])
+                in_g[h] = jnp.zeros_like(in_g[h])
 
             @pl.when(level < levels - 1)
             def _():
                 cotan_copy(h).wait_recv()
                 cotan = in_g[h]
-                out_g[team - 1, h] = cotan
 
                 @pl.when(level > 0)
                 def _():
@@ -327,9 +353,14 @@
             def _():
                 cotan_copy(h).start()
 
-        for j in range(team - 1, 0, -1):
+        cotans_at = [in_g[h] for h in range(mine_heads)]
+        for j in range(team - 1, -1, -1):
             for h in range(mine_heads):
-                out_g[j - 1, h] = mm(gt[j, h], out_g[j, h], ta=True) + ga[j, h]
+                out_g[j, h] = cotans_at[h].astype(LINK)
+                if j:
+                    cotans_at[h] = mm(gt[j, h].astype(F32), cotans_at[h], ta=True) + ga[
+                        j, h
+                    ].astype(F32)
 
         for other in others:
             give(other, mine, *cotans).start()
@@ -350,8 +381,8 @@
         give(mine, other, *states).wait_recv()
     for other in others:
         give(mine, other, *cotans).wait_recv()
-    state_ref[...] = back_s[...]
-    cotan_ref[...] = back_g[...]
+    state_ref[...] = back_s[...].astype(F32)
+    cotan_ref[...] = back_g[...].astype(F32)
     for other in others:
         for kind in kinds:
             spread(mine, other, *kind).wait_send()
@@ -365,6 +396,11 @@
         @pl.when(level > 0)
         def _():
             cotan_copy(h).wait_send()
+
+    @pl.when(me < n - 1)
+    def _():
+        for j, ref in enumerate((q_ref, k_ref, v_ref)):
+            halo_copy(j, ref).wait_send()
 
 
 def grads_kernel(
@@ -578,9 +614,6 @@
     steps = heads // group
     span = group * width
     dlog = decay_log.reshape(1, channels)
-    edges = jnp.stack([x[size - PAD :] for x in (query_raw, key_raw, value_raw)])
-    halo = lax.ppermute(edges, "seq", [(i, i + 1) for i in range(n - 1)])
-
     vmem = pl.BlockSpec(memory_space=pltpu.VMEM)
     tokens = pl.BlockSpec((size, span), lambda h: (0, h))
     rows8 = pl.BlockSpec((3, PAD, span), lambda h: (0, 0, h))
@@ -593,41 +626,41 @@
     sq = jax.ShapeDtypeStruct((heads, width, width), F32)
     pr = jax.ShapeDtypeStruct((heads, size, size), F32)
     tl = jax.ShapeDtypeStruct((heads, size, width), F32)
-    common = (query_raw, key_raw, value_raw, halo, gate_raw, beta_raw, conv_weight, dlog, grad_out)
+    params = pltpu.CompilerParams(vmem_limit_bytes=VMEM_LIMIT)
+    team = math.gcd(TEAM, math.gcd(n, heads))
+    part = heads // team
+    block = GROUP_MAPS if heads % GROUP_MAPS == 0 and GROUP_MAPS % part == 0 else heads
+    whole = pltpu.VMEM((heads, width, width), LINK)
+    few = pltpu.VMEM((part, width, width), F32)
+    many = pltpu.VMEM((team, part, width, width), LINK)
+    wide = pltpu.VMEM((team, part, width, width), F32)
+    sems = pltpu.SemaphoreType.DMA((team,))
+    hops = pltpu.SemaphoreType.DMA((part,))
+    three = pltpu.SemaphoreType.DMA((3,))
+    head_args = (query_raw, key_raw, value_raw)
+    tail_args = (gate_raw, beta_raw, conv_weight, dlog, grad_out)
+    halo, inv, raw, att, reach, state, cotan = pl.pallas_call(
+        functools.partial(scan_kernel, block),
+        out_shape=(
+            jax.ShapeDtypeStruct((3, PAD, channels), query_raw.dtype), pr, pr, pr, tl, sq, sq,
+        ),
+        in_specs=[vmem] * 8,
+        out_specs=(vmem,) * 7,
+        scratch_shapes=[
+            pltpu.VMEM((3 * block, PAD + size, width), F32),
+            pltpu.VMEM((3, PAD, channels), query_raw.dtype),
+        ]
+        + [whole] * 3 + [many] * 3 + [wide] * 2 + [few] * 4 + [many] * 2 + [whole] * 2
+        + [three] * 2 + [sems] * 6 + [hops] * 4 + [sems] * 4,
+        compiler_params=pltpu.CompilerParams(
+            collective_id=0, has_side_effects=True, vmem_limit_bytes=VMEM_LIMIT
+        ),
+        name="scan",
+    )(*head_args, *tail_args)
+    common = head_args + (halo,) + tail_args
     common_specs = [
         tokens, tokens, tokens, rows8, tokens, betas, weights, single, tokens,
     ]
-    params = pltpu.CompilerParams(vmem_limit_bytes=VMEM_LIMIT)
-    trans, offset, adjoint, inv, raw, att, reach = pl.pallas_call(
-        functools.partial(maps_kernel, group),
-        grid=(steps,),
-        out_shape=(sq, sq, sq, pr, pr, pr, tl),
-        in_specs=common_specs,
-        out_specs=(square, square, square, pairs, pairs, pairs, tall),
-        scratch_shapes=[pltpu.VMEM((3 * group, PAD + size, width), F32)],
-        compiler_params=params,
-        name="maps",
-    )(*common)
-
-    team = math.gcd(TEAM, math.gcd(n, heads))
-    part = heads // team
-    whole = pltpu.VMEM((heads, width, width), F32)
-    few = pltpu.VMEM((part, width, width), F32)
-    many = pltpu.VMEM((team, part, width, width), F32)
-    sems = pltpu.SemaphoreType.DMA((team,))
-    hops = pltpu.SemaphoreType.DMA((part,))
-    state, cotan = pl.pallas_call(
-        chain_kernel,
-        out_shape=(sq, sq),
-        in_specs=[vmem] * 3,
-        out_specs=(vmem, vmem),
-        scratch_shapes=[many] * 5 + [few] * 4 + [many] * 2 + [whole] * 2
-        + [sems] * 6 + [hops] * 4 + [sems] * 4,
-        compiler_params=pltpu.CompilerParams(
-            collective_id=0, has_side_effects=True, vmem_limit_bytes=VMEM_LIMIT
-        ),
-        name="chain",
-    )(trans, offset, adjoint)
 
     act = jax.ShapeDtypeStruct((size, channels), BF16)
     edge = jax.ShapeDtypeStruct((3, PAD, channels), F32)

time: 96.9 us -> 87.1 us (0.90)
  starting transfers between devices: 4.87 us -> 0 us
  Pallas kernels: 82.5 us -> 80.1 us
  local copies, waits for them, and re-layouts: 6.37 us -> 4.97 us
  waiting for transfers between devices: 1 us -> 0 us
    ppermute x1 -> x0, starting transfers between devices: 4.87 us -> none  [per_device(): halo = lax.ppermute(edges, 'seq', [(i, i + 1) for i in range(n - 1)])]
    pallas_call x2 -> x1, Pallas kernels: 55 us -> 52.4 us  [per_device(): pl.pallas_call(functools.partial(scan_kernel, block), out_shape=(jax.Shap...]
    another operation x2 -> x0, local copies, waits for them, and re-layouts: 1.46 us -> none  [per_device(): edges = jnp.stack([x[size - PAD:] for x in (query_raw, key_raw, value_raw)])]
    ppermute x1 -> x0, waiting for transfers between devices: 1 us -> none  [per_device(): halo = lax.ppermute(edges, 'seq', [(i, i + 1) for i in range(n - 1)])]
    unnamed x14 -> x10, local copies, waits for them, and re-layouts: 4.28 us -> 4.35 us
  transfers between devices with their start and end apart: 1 -> 0, of which waited for: 1 -> 0; matrix products, arithmetic and copies ran while one was open for 1% -> 0% of each run, Pallas kernels for 0% -> 0%
where the time goes in v2:
time: 87.1 us; the launch traced here: 86.7 us
  Pallas kernels  80.1 us (92%)
  local copies, waits for them, and re-layouts  4.97 us (6%)
  other arithmetic  0.91 us (1%)
    pallas_call x1, Pallas kernels, per_device(): pl.pallas_call(functools.partial(scan_kernel, block), out_shape=(jax.Shap...  52.4 us
    pallas_call x1, Pallas kernels, per_device(): pl.pallas_call(finish_kernel, out_shape=(jax.ShapeDtypeStruct(conv_weight...  15 us
    pallas_call x1, Pallas kernels, per_device(): pl.pallas_call(functools.partial(grads_kernel, group), grid=(steps,), out...  12.7 us
    unnamed x10, local copies, waits for them, and re-layouts  4.35 us

profile of v2, /device:TPU:0, one launch (start us, length us, event | category | flops | bytes accessed | tf_op | source)
XLA Modules:
  0.0 86.7 jit_solution(17507373896699427958)
XLA Ops:
  0.6 1.4 %copy.15.beta_ref = f32[128,8]{1,0:T(8,128)} copy(f32[128,8]{0,1:T(8,128)} %param.12) | data formatting | bytes 8192 | tf_op args[4]
  2.0 52.4 %scan.1 = (bf16[3,8,1024]{2,1,0:T(8,128)(2,1)}, f32[8,128,128]{2,1,0:T(8,128)}, f32[8,128,128]{2,1,0:T(8,128)}, f32[8,128,128]{2,1,0:T(8,128)}, f32[8,128,128]{2...) custom-call(bf16[128,1024]{1,0:T(8,128)(2,1)} %q_ref.3, bf16[128,1024]{1,0:T(8,128)(2,1)} %k_ref.3, ...), custom_call_target="tpu_custom_call" | custom-call | tf_op jit(solution)/shard_map/scan/pallas_call | solution.py:642
  54.5 12.7 %grads.1 = (bf16[128,1024]{1,0:T(8,128)(2,1)}, bf16[128,1024]{1,0:T(8,128)(2,1)}, bf16[128,1024]{1,0:T(8,128)(2,1)}, f32[128,1024]{1,0:T(8,128)}, f32[128,8]{1,0...) custom-call(bf16[128,1024]{1,0:T(8,128)(2,1)} %q_ref.3, bf16[128,1024]{1,0:T(8,128)(2,1)} %k_ref.3, ...), custom_call_target="tpu_custom_call" | custom-call | tf_op jit(solution)/shard_map/grads/pallas_call | solution.py:667
  67.2 1.5 %copy.17 = f32[128,8]{0,1:T(8,128)} copy(f32[128,8]{1,0:T(8,128)} %get-tuple-element.47) | data formatting | bytes 8192
  68.7 0.0 copy-start
  68.7 15.0 %finish.1 = (f32[3,4,1024]{2,1,0:T(4,128)}, f32[1,1024]{1,0:T(1,128)}, f32[3,8,1024]{2,1,0:T(8,128)}) custom-call(f32[128,128]{1,0:T(8,128)} %get-tuple-element.34.red_ref, f32[3,8,1024]{2,1,0:T(8,128)} %get-tuple-element.35.tail_ref), custom_call_target="tpu_custom_call" | custom-call | tf_op jit(solution)/shard_map/finish/pallas_call | solution.py:693
  83.7 0.0 copy-done
  83.7 0.9 %add_convert_fusion = bf16[3,8,1024]{2,1,0:T(8,128)(2,1)S(1)} fusion(f32[3,8,1024]{2,1,0:T(8,128)S(1)} %copy-done, f32[3,8,1024]{2,1,0:T(8,128)} %get-tuple-element.36), kind=kLoop, calls=%fused_computation | loop fusion | flops 49152 | bytes 245760 | tf_op jit(solution)/shard_map/convert_element_type | solution.py:720
  84.6 0.0 copy-start.1
  84.6 0.6 fusion
  85.3 0.2 copy-done.1
  85.4 0.0 copy-start.2
  85.4 0.6 copy.23
  86.0 0.1 copy-done.2
  86.1 0.6 copy.24
Async XLA Ops:
  68.7 15.0 %copy-start = (f32[3,8,1024]{2,1,0:T(8,128)S(1)}, f32[3,8,1024]{2,1,0:T(8,128)}, u32[]{:S(2)}) copy-start(f32[3,8,1024]{2,1,0:T(8,128)} %get-tuple-element.33) | copy-start | bytes 294916
  84.6 0.8 copy-start.1
  85.4 0.7 copy-start.2

commit v3 on v2

--- a/solution.py
+++ b/solution.py
@@ -83,9 +83,9 @@
 
 
 def pick_column(ref, index):
-    block = ref[...]
-    lane = lax.broadcasted_iota(jnp.int32, block.shape, 1)
-    return jnp.sum(jnp.where(lane == index, block, 0.0), axis=1, keepdims=True)
+    row = ref[pl.ds(index, 1), :]
+    r, c = iotas(row.shape[1])
+    return jnp.sum(jnp.where(r == c, row, 0.0), axis=1, keepdims=True)
 
 
 def unit(x):
@@ -473,8 +473,9 @@
         dgate_ref[:, cols] = speed * sigmoid(gate) * d_ld
         d_dlog = jnp.sum(ld * d_ld, axis=0, keepdims=True)
         d_braw = d_beta * beta * (1.0 - beta)
-        lane = lax.broadcasted_iota(jnp.int32, dbeta_ref.shape, 1)
-        dbeta_ref[...] = jnp.where(lane == head, d_braw, dbeta_ref[...])
+        dbeta_ref[pl.ds(head, 1), :] = jnp.sum(
+            jnp.where(r == c, d_braw, 0.0), axis=0, keepdims=True
+        )
 
         d_q = q_r * (d_q - q * jnp.sum(q * d_q, axis=1, keepdims=True))
         d_k = k_r * (d_k - k * jnp.sum(k * d_k, axis=1, keepdims=True))
@@ -617,7 +618,7 @@
     vmem = pl.BlockSpec(memory_space=pltpu.VMEM)
     tokens = pl.BlockSpec((size, span), lambda h: (0, h))
     rows8 = pl.BlockSpec((3, PAD, span), lambda h: (0, 0, h))
-    betas = pl.BlockSpec((size, heads), lambda h: (0, 0))
+    betas = pl.BlockSpec((heads, size), lambda h: (0, 0))
     weights = pl.BlockSpec((3, conv_weight.shape[1], span), lambda h: (0, 0, h))
     single = pl.BlockSpec((1, span), lambda h: (0, h))
     square = pl.BlockSpec((group, width, width), lambda h: (h, 0, 0))
@@ -638,7 +639,7 @@
     hops = pltpu.SemaphoreType.DMA((part,))
     three = pltpu.SemaphoreType.DMA((3,))
     head_args = (query_raw, key_raw, value_raw)
-    tail_args = (gate_raw, beta_raw, conv_weight, dlog, grad_out)
+    tail_args = (gate_raw, beta_raw.T, conv_weight, dlog, grad_out)
     halo, inv, raw, att, reach, state, cotan = pl.pallas_call(
         functools.partial(scan_kernel, block),
         out_shape=(
@@ -670,7 +671,7 @@
         out_shape=(
             act, act, act,
             jax.ShapeDtypeStruct((size, channels), F32),
-            jax.ShapeDtypeStruct((size, heads), F32),
+            jax.ShapeDtypeStruct((heads, size), F32),
             jax.ShapeDtypeStruct((heads * RED, width), F32),
             edge, edge,
         ),
@@ -721,7 +722,7 @@
     dq = lax.dynamic_update_slice(dq, ends[0], (size - PAD, 0))
     dk = lax.dynamic_update_slice(dk, ends[1], (size - PAD, 0))
     dv = lax.dynamic_update_slice(dv, ends[2], (size - PAD, 0))
-    return (dq, dk, dv, dgate, dbeta, conv_sum, decay_sum.reshape(channels))
+    return (dq, dk, dv, dgate, dbeta.T, conv_sum, decay_sum.reshape(channels))
 
 
 def solution(mesh):

time: 87.1 us -> 84.1 us (0.966)
  local copies, waits for them, and re-layouts: 4.97 us -> 2.06 us
    unnamed x10 -> x8, local copies, waits for them, and re-layouts: 4.35 us -> 1.44 us
where the time goes in v3:
time: 84.1 us; the launch traced here: 83.8 us
  Pallas kernels  80.1 us (95%)
  local copies, waits for them, and re-layouts  2.06 us (2%)
  other arithmetic  0.91 us (1%)
    pallas_call x1, Pallas kernels, per_device(): pl.pallas_call(functools.partial(scan_kernel, block), out_shape=(jax.Shap...  52.5 us
    pallas_call x1, Pallas kernels, per_device(): pl.pallas_call(finish_kernel, out_shape=(jax.ShapeDtypeStruct(conv_weight...  15 us
    pallas_call x1, Pallas kernels, per_device(): pl.pallas_call(functools.partial(grads_kernel, group), grid=(steps,), out...  12.7 us

profile of v3, /device:TPU:0, one launch (start us, length us, event | category | flops | bytes accessed | tf_op | source)
XLA Modules:
  0.0 83.8 jit_solution(7329922464065297071)
XLA Ops:
  0.6 52.5 %scan.1 = (bf16[3,8,1024]{2,1,0:T(8,128)(2,1)}, f32[8,128,128]{2,1,0:T(8,128)}, f32[8,128,128]{2,1,0:T(8,128)}, f32[8,128,128]{2,1,0:T(8,128)}, f32[8,128,128]{2...) custom-call(bf16[128,1024]{1,0:T(8,128)(2,1)} %q_ref.3, bf16[128,1024]{1,0:T(8,128)(2,1)} %k_ref.3, ...), custom_call_target="tpu_custom_call" | custom-call | tf_op jit(solution)/shard_map/scan/pallas_call | solution.py:643
  53.1 12.7 %grads.1 = (bf16[128,1024]{1,0:T(8,128)(2,1)}, bf16[128,1024]{1,0:T(8,128)(2,1)}, bf16[128,1024]{1,0:T(8,128)(2,1)}, f32[128,1024]{1,0:T(8,128)}, f32[8,128]{1,0...) custom-call(bf16[128,1024]{1,0:T(8,128)(2,1)} %q_ref.3, bf16[128,1024]{1,0:T(8,128)(2,1)} %k_ref.3, ...), custom_call_target="tpu_custom_call" | custom-call | tf_op jit(solution)/shard_map/grads/pallas_call | solution.py:668
  65.8 0.0 copy-start
  65.8 15.0 %finish.1 = (f32[3,4,1024]{2,1,0:T(4,128)}, f32[1,1024]{1,0:T(1,128)}, f32[3,8,1024]{2,1,0:T(8,128)}) custom-call(f32[128,128]{1,0:T(8,128)} %get-tuple-element.34.red_ref, f32[3,8,1024]{2,1,0:T(8,128)} %get-tuple-element.35.tail_ref), custom_call_target="tpu_custom_call" | custom-call | tf_op jit(solution)/shard_map/finish/pallas_call | solution.py:694
  80.8 0.0 copy-done
  80.8 0.9 %add_convert_fusion = bf16[3,8,1024]{2,1,0:T(8,128)(2,1)S(1)} fusion(f32[3,8,1024]{2,1,0:T(8,128)S(1)} %copy-done, f32[3,8,1024]{2,1,0:T(8,128)} %get-tuple-element.36), kind=kLoop, calls=%fused_computation | loop fusion | flops 49152 | bytes 245760 | tf_op jit(solution)/shard_map/convert_element_type | solution.py:721
  81.7 0.0 copy-start.1
  81.7 0.6 fusion
  82.3 0.2 copy-done.1
  82.5 0.0 copy-start.2
  82.5 0.6 copy.20
  83.1 0.1 copy-done.2
  83.2 0.6 copy.21
Async XLA Ops:
  65.8 15.0 %copy-start = (f32[3,8,1024]{2,1,0:T(8,128)S(1)}, f32[3,8,1024]{2,1,0:T(8,128)}, u32[]{:S(2)}) copy-start(f32[3,8,1024]{2,1,0:T(8,128)} %get-tuple-element.33) | copy-start | bytes 294916
  81.7 0.8 copy-start.1
  82.5 0.7 copy-start.2
